TPU v7x, 256 devices: a whole 4x4x8 slice. The times are simulated.
256 devices in a mesh: src: 8 (over y, core), tgt: 32 (over z, x).
Axes of the slice: x: 4, y: 4, z: 8, core: 2. Of those that a mesh axis runs over, the one named last changes fastest.
Arguments:
- src_embed: bfloat16 [8192, 256], P('src'), may hold values from -128 to 128
- tgt_embed: bfloat16 [155648, 256], P('tgt'), may hold values from -1 to 1
- qwen_embed: bfloat16 [155648, 256], P('tgt'), may hold values from -6 to 6
- other_log: float32 [155648], P('tgt'), may hold values from -12 to -10
- src_counts: int32 [8192], P('src'), may hold values from 1 to 999
- tgt_counts: int32 [155648], P('tgt'), may hold values from 1 to 999
Outputs:
- transported: float32 [8192, 256], P(('src', 'tgt'))
All inputs are finite; a program needn't handle non-finite values.
Results may differ from a plain program's by a relative error of at most 0.0034.
Values sent between devices are 32-bit elements; how exact they have to be, the bound alone decides.
A program may use at most 128 MiB of HBM per device.

v0:
```python
import jax
import jax.numpy as jnp
from jax import lax
from jax.sharding import PartitionSpec as P

ITERS = 2


inv_temp = 4.0


def logits_of(src_embed, tgt_embed):
    products = lax.dot_general(
        src_embed, tgt_embed, (((1,), (1,)), ((), ())), preferred_element_type=jnp.float32
    )
    return products * inv_temp


def row_lse(values):
    local_peak = jnp.max(values, axis=1)
    peak = lax.pmax(local_peak, "tgt")
    total = lax.psum(jnp.sum(jnp.exp(values - peak[:, None]), axis=1), "tgt")
    return peak + jnp.log(total)


def col_lse(values):
    local_peak = jnp.max(values, axis=0)
    peak = lax.pmax(local_peak, "src")
    total = lax.psum(jnp.sum(jnp.exp(values - peak[None, :]), axis=0), "src")
    return peak + jnp.log(total)


def on_device(src_embed, tgt_embed, qwen_embed, other_log, src_counts, tgt_counts):
    src_float = src_counts.astype(jnp.float32)
    tgt_float = tgt_counts.astype(jnp.float32)
    slab_sum = lax.psum(jnp.sum(src_float), "src")
    vocab_sum = lax.psum(jnp.sum(tgt_float), "tgt")
    src_log = jnp.log(src_float) - jnp.log(slab_sum)
    tgt_log = jnp.log(tgt_float) - jnp.log(vocab_sum)
    stored = logits_of(src_embed, tgt_embed)

    def current():
        return stored

    col_pot = jnp.zeros((tgt_embed.shape[0],), jnp.float32)
    row_pot = jnp.zeros((src_embed.shape[0],), jnp.float32)
    for sweep in range(ITERS):
        row_pot = src_log - row_lse(current() + col_pot[None, :])
        col_pot = tgt_log - jnp.logaddexp(col_lse(current() + row_pot[:, None]), other_log)
    shift = row_pot - src_log
    weights = jnp.exp(shift[:, None] + col_pot[None, :] + current()).astype(jnp.bfloat16)
    owned_rows = src_embed.shape[0] // lax.axis_size("tgt")
    partial_rows = jnp.dot(weights, qwen_embed, preferred_element_type=jnp.float32)
    summed = lax.psum(partial_rows, "tgt")
    return lax.dynamic_slice_in_dim(summed, lax.axis_index("tgt") * owned_rows, owned_rows, 0)


def solution(mesh):
    return jax.shard_map(
        on_device,
        mesh=mesh,
        in_specs=(P("src", None), P("tgt", None), P("tgt", None), P("tgt"), P("src"), P("tgt")),
        out_specs=P(("src", "tgt"), None),
        check_vma=False,
    )
```

profile of v0, /device:TPU:32, one launch (start us, length us, event | category | flops | bytes accessed | tf_op | source)
XLA Modules:
  0.0 645.6 jit_solution(11345955397474943461)
XLA Ops:
  6.5 0.0 copy-start
  6.5 0.0 all-reduce.3.cloned.1.call-start
  6.5 1.5 convert_reduce_fusion
  8.0 1.3 convert_reduce_fusion.1
  9.3 0.0 copy-done
  9.3 0.0 copy-start.3
  9.3 9.3 %fusion.4 = (f32[1024]{0:T(1024)S(1)}, f32[1024,4864]{1,0:T(8,128)}) fusion(bf16[1024,256]{1,0:T(8,128)(2,1)} %param.6, bf16[4864,256]{1,0:T(8,128)(2,1)S(1)} %copy-done), kind=kOutput, calls=%fused_computation.24 | convolution fusion | flops 2560097280 | bytes 22941696 | tf_op jit(solution)/shard_map/dot_general | solution.py:13
  18.7 71.2 %pmax.28 = f32[1024]{0:T(1024)S(1)} all-reduce(f32[1024]{0:T(1024)S(1)} %get-tuple-element.9), channel_id=1, replica_groups=mesh['src'=8,'tgt'=32] {'tgt'}, use_global_device_ids=true, to_apply=%region_5.0 | all-reduce | flops 1024 | bytes 8192 | tf_op jit(solution)/shard_map/pmax | solution.py:21
  89.8 13.0 %psum.49 = f32[]{:T(128)} all-reduce(f32[]{:T(128)} %convert_reduce_fusion.1), channel_id=1, replica_groups=mesh['src'=8,'tgt'=32] {'src'}, use_global_device_ids=true, to_apply=%region_1.0 | all-reduce | flops 1 | bytes 8 | tf_op jit(solution)/shard_map/psum | solution.py:36
  103.6 9.4 %exponential_reduce_fusion.3 = f32[1024]{0:T(1024)S(1)} fusion(f32[1024,4864]{1,0:T(8,128)} %get-tuple-element.10, f32[1024]{0:T(1024)S(1)} %pmax.28), kind=kLoop, calls=%fused_computation.4 | loop fusion | flops 9960448 | bytes 19931136 | tf_op jit(solution)/shard_map/reduce_sum | solution.py:22
  113.0 71.2 %all-reduce = (f32[1024]{0:T(1024)S(1)}, f32[]{:T(128)}) all-reduce(f32[1024]{0:T(1024)S(1)} %exponential_reduce_fusion.3, f32[]{:T(128)} %convert_reduce_fusion), channel_id=1, replica_groups=mesh['src'=8,'tgt'=32] {'tgt'}, use_global_device_ids=true, to_apply=%region_7.0 | all-reduce | flops 1025 | bytes 8200 | tf_op jit(solution)/shard_map/psum | solution.py:22
  184.1 0.0 copy-done.3
  184.2 0.0 copy-start.1
  184.2 0.0 copy-start.2
  184.2 8.3 %add_reduce_fusion.2 = f32[4864]{0:T(1024)S(1)} fusion(f32[1024,4864]{1,0:T(8,128)} %get-tuple-element.10, f32[1024]{0:T(1024)S(1)} %add_subtract_fusion.1), kind=kLoop, calls=%fused_computation.7 | loop fusion | flops 9956608 | bytes 19946496 | tf_op jit(solution)/shard_map/reduce_max | solution.py:27
  192.5 23.6 %pmax.29 = f32[4864]{0:T(1024)S(1)} all-reduce(f32[4864]{0:T(1024)S(1)} %add_reduce_fusion.2), channel_id=1, replica_groups=mesh['src'=8,'tgt'=32] {'src'}, use_global_device_ids=true, to_apply=%region_9.0 | all-reduce | flops 4864 | bytes 38912 | tf_op jit(solution)/shard_map/pmax | solution.py:28
  216.1 10.9 %exponential_reduce_fusion.2 = f32[4864]{0:T(1024)S(1)} fusion(f32[1024,4864]{1,0:T(8,128)} %get-tuple-element.10, f32[4864]{0:T(1024)S(1)} %pmax.29, f32[1024]{0:T(1024)S(1)} %add_subtract_fusion.1), kind=kLoop, calls=%fused_computation.3 | loop fusion | flops 14937344 | bytes 19965952 | tf_op jit(solution)/shard_map/reduce_sum | solution.py:29
  226.9 23.8 %psum.52 = f32[4864]{0:T(1024)S(1)} all-reduce(f32[4864]{0:T(1024)S(1)} %exponential_reduce_fusion.2), channel_id=1, replica_groups=mesh['src'=8,'tgt'=32] {'src'}, use_global_device_ids=true, to_apply=%region_11.0 | all-reduce | flops 4864 | bytes 38912 | tf_op jit(solution)/shard_map/psum | solution.py:29
  251.4 0.0 copy-done.1
  251.4 0.0 copy-done.2
  251.5 8.1 %add_reduce_fusion.1 = f32[1024]{0:T(1024)S(1)} fusion(f32[1024,4864]{1,0:T(8,128)} %get-tuple-element.10, f32[4864]{0:T(1024)S(1)} %select_subtract_fusion.1), kind=kLoop, calls=%fused_computation.6 | loop fusion | flops 9960448 | bytes 19946496 | tf_op jit(solution)/shard_map/reduce_max | solution.py:20
  259.5 71.6 %pmax.30 = f32[1024]{0:T(1024)S(1)} all-reduce(f32[1024]{0:T(1024)S(1)} %add_reduce_fusion.1), channel_id=1, replica_groups=mesh['src'=8,'tgt'=32] {'tgt'}, use_global_device_ids=true, to_apply=%region_13.0 | all-reduce | flops 1024 | bytes 8192 | tf_op jit(solution)/shard_map/pmax | solution.py:21
  331.1 10.0 %exponential_reduce_fusion.1 = f32[1024]{0:T(1024)S(1)} fusion(f32[1024,4864]{1,0:T(8,128)} %get-tuple-element.10, f32[1024]{0:T(1024)S(1)} %pmax.30, f32[4864]{0:T(1024)S(1)} %select_subtract_fusion.1), kind=kLoop, calls=%fused_computation.2 | loop fusion | flops 14941184 | bytes 19950592 | tf_op jit(solution)/shard_map/reduce_sum | solution.py:22
  341.2 69.7 %psum.53 = f32[1024]{0:T(1024)S(1)} all-reduce(f32[1024]{0:T(1024)S(1)} %exponential_reduce_fusion.1), channel_id=1, replica_groups=mesh['src'=8,'tgt'=32] {'tgt'}, use_global_device_ids=true, to_apply=%region_15.0 | all-reduce | flops 1024 | bytes 8192 | tf_op jit(solution)/shard_map/psum | solution.py:22
  410.8 8.3 %add_reduce_fusion = f32[4864]{0:T(1024)S(1)} fusion(f32[1024,4864]{1,0:T(8,128)} %get-tuple-element.10, f32[1024]{0:T(1024)S(1)} %get-tuple-element.8), kind=kLoop, calls=%fused_computation.5 | loop fusion | flops 9956608 | bytes 19946496 | tf_op jit(solution)/shard_map/reduce_max | solution.py:27
  419.1 23.6 %pmax.31 = f32[4864]{0:T(1024)S(1)} all-reduce(f32[4864]{0:T(1024)S(1)} %add_reduce_fusion), channel_id=1, replica_groups=mesh['src'=8,'tgt'=32] {'src'}, use_global_device_ids=true, to_apply=%region_17.0 | all-reduce | flops 4864 | bytes 38912 | tf_op jit(solution)/shard_map/pmax | solution.py:28
  442.7 10.9 %exponential_reduce_fusion = f32[4864]{0:T(1024)S(1)} fusion(f32[1024,4864]{1,0:T(8,128)} %get-tuple-element.10, f32[4864]{0:T(1024)S(1)} %pmax.31, f32[1024]{0:T(1024)S(1)} %get-tuple-element.8), kind=kLoop, calls=%fused_computation.1 | loop fusion | flops 14937344 | bytes 19965952 | tf_op jit(solution)/shard_map/reduce_sum | solution.py:29
  453.6 23.8 %psum.54 = f32[4864]{0:T(1024)S(1)} all-reduce(f32[4864]{0:T(1024)S(1)} %exponential_reduce_fusion), channel_id=1, replica_groups=mesh['src'=8,'tgt'=32] {'src'}, use_global_device_ids=true, to_apply=%region_19.0 | all-reduce | flops 4864 | bytes 38912 | tf_op jit(solution)/shard_map/psum | solution.py:29
  477.5 11.5 %fusion = f32[1024,256]{1,0:T(8,128)} fusion(bf16[4864,256]{1,0:T(8,128)(2,1)} %param.8, f32[1024,4864]{1,0:T(8,128)} %get-tuple-element.10, f32[4864]{0:T(1024)S(1)} %select_subtract_fusion, f32[1024]{0:T(1024)S(1)} %get-tuple-element.7), kind=kOutput, calls=%fused_computation.9 | convolution fusion | flops 2565079040 | bytes 23485440 | tf_op jit(solution)/shard_map/dot_general | solution.py:53
  489.0 0.0 all-reduce.3.cloned.1.call-update
  489.0 148.3 %all-reduce.3.cloned.1.call-done = f32[1024,256]{1,0:T(8,128)} async-done(((f32[1024,256]{1,0:T(8,128)}), f32[1024,256]{1,0:T(8,128)}) %all-reduce.3.cloned.1.call-update) | async-done | bytes 1048592 | tf_op jit(solution)/shard_map/psum | solution.py:54
  637.3 1.4 constant_dynamic-slice_fusion
  (4 shorter events, 0.1 us)
Async XLA Ops:
  6.5 2.8 copy-start
  6.5 630.8 %all-reduce.3.cloned.1.call-start = ((), (), s32[]{:S(2)}) async-start(), calls=%async_computation | async-start | bytes 2097152 | tf_op jit(solution)/shard_map/psum | solution.py:54
  9.3 174.8 %copy-start.3 = (s32[1024]{0:T(1024)S(1)}, s32[1024]{0:T(1024)}, u32[]{:S(2)}) copy-start(s32[1024]{0:T(1024)} %param.10) | copy-start | bytes 12292
  184.2 67.3 %copy-start.1 = (s32[4864]{0:T(1024)S(1)}, s32[4864]{0:T(1024)}, u32[]{:S(2)}) copy-start(s32[4864]{0:T(1024)} %param.11) | copy-start | bytes 58372
  184.2 67.3 %copy-start.2 = (f32[4864]{0:T(1024)S(1)}, f32[4864]{0:T(1024)}, u32[]{:S(2)}) copy-start(f32[4864]{0:T(1024)} %param.9) | copy-start | bytes 58372
Sparse Core Ops, SparseCore 0:
  489.1 148.1 all-reduce.2
where the time goes:
time: 647 us; the launch traced here: 646 us
  blocking collectives  391 us (60%)
  waiting for transfers between devices  148 us (23%)
  other arithmetic  68.7 us (11%)
  matrix products  20.9 us (3%)
  between operations  14.8 us (2%)
    psum x1, waiting for transfers between devices, on_device(): summed = lax.psum(partial_rows, 'tgt')  148 us
    pmax x2, blocking collectives, row_lse(): peak = lax.pmax(local_peak, 'tgt')  143 us
    psum x2, blocking collectives, row_lse(): total = lax.psum(jnp.sum(jnp.exp(values - peak[:, None]), axis=1), 'tgt')  141 us
    psum x2, blocking collectives, col_lse(): total = lax.psum(jnp.sum(jnp.exp(values - peak[None, :]), axis=0), 'src')  47.6 us
    pmax x2, blocking collectives, col_lse(): peak = lax.pmax(local_peak, 'src')  47.2 us
    reduce_sum x2, other arithmetic, col_lse(): total = lax.psum(jnp.sum(jnp.exp(values - peak[None, :]), axis=0), 'src')  21.7 us
    reduce_sum x2, other arithmetic, row_lse(): total = lax.psum(jnp.sum(jnp.exp(values - peak[:, None]), axis=1), 'tgt')  19.4 us
    reduce_max x2, other arithmetic, col_lse(): local_peak = jnp.max(values, axis=0)  16.6 us
  transfers between devices with their start and end apart: 1, of which 1 were waited for; matrix products, arithmetic and copies ran while one was open for 0% of the time, Pallas kernels for 0%

commit v1 on v0

v1 whole, which is shorter than its diff:
```python
import functools
import math

import jax
import jax.numpy as jnp
from jax import lax
from jax.experimental import pallas as pl
from jax.experimental.pallas import tpu as pltpu
from jax.sharding import PartitionSpec as P

MESH = pl.DeviceIdType.MESH
LANES = 128
NX = 4
SCALE = 4.0 * math.log2(math.e)
NT = (((1,), (1,)), ((), ()))
NN = (((1,), (0,)), ((), ()))


def dot(a, b, dims):
    return lax.dot_general(a, b, dims, preferred_element_type=jnp.float32)


def kernel(
    n_src, n_tgt,
    src_hbm, tgt_hbm, qwen_hbm, other_ref, src_counts_ref, tgt_counts_ref,
    out_ref,
    src_v, tgt_v, qwen_v, qt_v, logit_v, kt_v, row_lhs, col_lhs,
    r1_send, r1_recv, c1_send, c1_recv, r2_send, r2_recv, c2_send, c2_recv,
    f_send, f_recv, g_send, g_recv,
    load_sem, send_sem, recv_sem,
):
    rows, emb = src_v.shape
    cols = tgt_v.shape[0]
    n_z = n_tgt // NX
    row_tiles, col_tiles = rows // LANES, cols // LANES
    owned = rows // n_tgt
    me_src, me_tgt = lax.axis_index("src"), lax.axis_index("tgt")
    me_z, me_x = me_tgt // NX, me_tgt % NX

    loads = [
        pltpu.make_async_copy(src_hbm, src_v, load_sem.at[0]),
        pltpu.make_async_copy(tgt_hbm, tgt_v, load_sem.at[1]),
        pltpu.make_async_copy(qwen_hbm, qwen_v, load_sem.at[2]),
    ]
    for load in loads:
        load.start()

    tgt_peers = [(me_src, (me_tgt + d) % n_tgt) for d in range(1, n_tgt)]
    src_peers = [((me_src + d) % n_src, me_tgt) for d in range(1, n_src)]
    barrier = pltpu.get_barrier_semaphore()
    for peer in tgt_peers + src_peers:
        pl.semaphore_signal(barrier, inc=1, device_id=peer, device_id_type=MESH)

    def start(send_ref, recv_ref, k, peers):
        for slot, peer in enumerate(peers):
            pltpu.make_async_remote_copy(
                src_ref=send_ref, dst_ref=recv_ref.at[slot],
                send_sem=send_sem.at[k], recv_sem=recv_sem.at[k],
                device_id=peer, device_id_type=MESH,
            ).start()

    def wait_recv(recv_ref, k):
        pltpu.make_async_copy(recv_ref, recv_ref, recv_sem.at[k]).wait()

    def wait_send(recv_ref, k):
        pltpu.make_async_copy(recv_ref, recv_ref, send_sem.at[k]).wait()

    loads[0].wait()
    loads[1].wait()
    width, block = 256, 608 if cols % 608 == 0 else cols
    n_blocks = cols // block
    for i in range(rows // width):
        lanes = pl.ds(i * width, width)
        src_part = src_v[lanes, :]

        def products(b, peak):
            js = pl.ds(pl.multiple_of(b * block, block), block)
            d = dot(tgt_v[js, :], src_part, NT)
            logit_v[js, :] = d
            return jnp.maximum(peak, jnp.max(d.reshape(block // 8, 8, width), axis=0))

        peak = lax.fori_loop(0, n_blocks, products, jnp.full((8, width), -3.0e38, jnp.float32))
        peak = jnp.max(peak, axis=0, keepdims=True)

        def exponentials(b, total):
            js = pl.ds(pl.multiple_of(b * block, block), block)
            e = jnp.exp2((logit_v[js, :] - peak) * SCALE)
            kt_v[js, lanes] = e.astype(jnp.bfloat16)
            return total + jnp.sum(e.reshape(block // 8, 8, width), axis=0)

        total = lax.fori_loop(0, n_blocks, exponentials, jnp.zeros((8, width), jnp.float32))
        total = jnp.sum(total, axis=0, keepdims=True)
        for h in range(width // LANES):
            t = i * (width // LANES) + h
            r1_send[t:t + 1, :] = peak[:, h * LANES:(h + 1) * LANES]
            r1_send[row_tiles + t:row_tiles + t + 1, :] = total[:, h * LANES:(h + 1) * LANES]

    pl.semaphore_wait(barrier, len(tgt_peers) + len(src_peers))
    start(r1_send, r1_recv, 0, tgt_peers)

    other_mass = jnp.exp(other_ref[...])
    src_counts = src_counts_ref[...].astype(jnp.float32)
    tgt_counts = tgt_counts_ref[...].astype(jnp.float32)
    row_lhs[...] = jnp.zeros_like(row_lhs)
    col_lhs[...] = jnp.zeros_like(col_lhs)
    loads[2].wait()

    def turn(b, carry):
        js = pl.ds(pl.multiple_of(b * 256, 256), 256)
        qt_v[:, js] = qwen_v[js, :].T
        return carry

    lax.fori_loop(0, cols // 256, turn, 0)

    def spread(lhs, dense, tiles):
        high = dense.astype(jnp.bfloat16).astype(jnp.float32)
        low = dense - high
        for t in range(tiles):
            lhs[0:1, t * LANES:(t + 1) * LANES] = high[t:t + 1, :]
            lhs[1:2, t * LANES:(t + 1) * LANES] = low[t:t + 1, :]

    def column_sums(dest):
        a = row_lhs[...].astype(jnp.bfloat16)

        for b in range(cols // 256):
            c = jnp.sum(dot(a, kt_v[b * 256:(b + 1) * 256, :], NT), axis=0, keepdims=True)
            for h in range(2):
                dest[2 * b + h:2 * b + h + 1, :] = c[:, h * LANES:(h + 1) * LANES]

    def row_sums():
        def body(b, acc):
            js = pl.ds(pl.multiple_of(b * 256, 256), 256)
            return acc + dot(col_lhs[:, js].astype(jnp.bfloat16), kt_v[js, :], NN)

        acc = lax.fori_loop(0, cols // 256, body, jnp.zeros((8, rows), jnp.float32))
        return jnp.sum(acc, axis=0, keepdims=True)

    wait_recv(r1_recv, 0)
    local_peak, local_total = r1_send[0:row_tiles, :], r1_send[row_tiles:2 * row_tiles, :]
    top = jnp.maximum(local_peak, jnp.max(r1_recv[:, 0:row_tiles, :], axis=0))
    factor = jnp.exp2((local_peak - top) * SCALE)
    mass = local_total * factor
    for d in range(n_tgt - 1):
        mass += r1_recv[d, row_tiles:2 * row_tiles, :] * jnp.exp2(
            (r1_recv[d, 0:row_tiles, :] - top) * SCALE
        )
    spread(row_lhs, src_counts / mass * factor, row_tiles)

    column_sums(c1_send)
    c1_send[col_tiles:, :] = jnp.full((2, LANES), jnp.sum(src_counts), jnp.float32)
    start(c1_send, c1_recv, 1, src_peers)
    r2_send[row_tiles:, :] = jnp.full((row_tiles, LANES), jnp.sum(tgt_counts), jnp.float32)
    wait_recv(c1_recv, 1)
    sums = c1_send[...] + jnp.sum(c1_recv[...], axis=0)
    slab_total = sums[col_tiles:col_tiles + 1, :]
    spread(col_lhs, tgt_counts / (sums[:col_tiles, :] / slab_total + other_mass), col_tiles)

    r = row_sums()
    for t in range(row_tiles):
        r2_send[t:t + 1, :] = r[:, t * LANES:(t + 1) * LANES] * factor[t:t + 1, :]
    start(r2_send, r2_recv, 2, tgt_peers)
    wait_recv(r2_recv, 2)
    sums = r2_send[...] + jnp.sum(r2_recv[...], axis=0)
    vocab_total = sums[row_tiles:, :]
    gain = factor / sums[:row_tiles, :]
    spread(row_lhs, src_counts / slab_total * vocab_total * gain, row_tiles)

    column_sums(c2_send)
    c2_send[col_tiles:, :] = jnp.zeros((2, LANES), jnp.float32)
    start(c2_send, c2_recv, 3, src_peers)
    wait_recv(c2_recv, 3)
    sums = c2_send[...] + jnp.sum(c2_recv[...], axis=0)
    spread(col_lhs, tgt_counts / (sums[:col_tiles, :] + other_mass), col_tiles)

    def weigh(b, carry):
        js = pl.ds(pl.multiple_of(b * 256, 256), 256)
        v = col_lhs[0:1, js] + col_lhs[1:2, js]
        qt_v[:, js] = (qt_v[:, js].astype(jnp.float32) * v).astype(jnp.bfloat16)
        return carry

    lax.fori_loop(0, cols // 256, weigh, 0)
    for i in range(rows // width):
        part = dot(qt_v[...], kt_v[:, i * width:(i + 1) * width], NN)
        for h in range(width // LANES):
            t = i * (width // LANES) + h
            turned = (part[:, h * LANES:(h + 1) * LANES] * gain[t:t + 1, :]).T
            f_send[t, :, :, :] = turned.reshape(NX, owned, turned.shape[1])

    for d in range(1, NX):
        peer_x = (me_x + d) % NX
        pltpu.make_async_remote_copy(
            src_ref=f_send.at[:, peer_x], dst_ref=f_recv.at[d - 1],
            send_sem=send_sem.at[4], recv_sem=recv_sem.at[4],
            device_id=(me_src, me_z * NX + peer_x), device_id_type=MESH,
        ).start()
    wait_recv(f_recv, 4)
    g_send[...] = f_send[:, me_x] + f_recv[0] + f_recv[1] + f_recv[2]
    for d in range(1, n_z):
        peer_z = (me_z + d) % n_z
        pltpu.make_async_remote_copy(
            src_ref=g_send.at[peer_z], dst_ref=g_recv.at[d - 1],
            send_sem=send_sem.at[5], recv_sem=recv_sem.at[5],
            device_id=(me_src, peer_z * NX + me_x), device_id_type=MESH,
        ).start()
    wait_recv(g_recv, 5)
    out_ref[...] = g_send[me_z] + jnp.sum(g_recv[...], axis=0)

    for k, recv_ref in enumerate((r1_recv, c1_recv, r2_recv, c2_recv, f_recv, g_recv)):
        wait_send(recv_ref, k)


def on_device(n_src, n_tgt, src_embed, tgt_embed, qwen_embed, other_log, src_counts, tgt_counts):
    rows, emb = src_embed.shape
    cols, dim = qwen_embed.shape
    row_tiles, col_tiles = rows // LANES, cols // LANES
    owned, n_z = rows // n_tgt, n_tgt // NX
    assert owned * NX == LANES
    f32, bf16 = jnp.float32, jnp.bfloat16
    vmem = pl.BlockSpec(memory_space=pltpu.VMEM)
    hbm = pl.BlockSpec(memory_space=pl.ANY)
    return pl.pallas_call(
        functools.partial(kernel, n_src, n_tgt),
        out_shape=jax.ShapeDtypeStruct((owned, dim), f32),
        in_specs=[hbm, hbm, hbm, vmem, vmem, vmem],
        out_specs=vmem,
        scratch_shapes=[
            pltpu.VMEM((rows, emb), bf16),
            pltpu.VMEM((cols, emb), bf16),
            pltpu.VMEM((cols, dim), bf16),
            pltpu.VMEM((dim, cols), bf16),
            pltpu.VMEM((cols, 256), f32),
            pltpu.VMEM((cols, rows), bf16),
            pltpu.VMEM((8, rows), f32),
            pltpu.VMEM((8, cols), f32),
            pltpu.VMEM((2 * row_tiles, LANES), f32),
            pltpu.VMEM((n_tgt - 1, 2 * row_tiles, LANES), f32),
            pltpu.VMEM((col_tiles + 2, LANES), f32),
            pltpu.VMEM((n_src - 1, col_tiles + 2, LANES), f32),
            pltpu.VMEM((2 * row_tiles, LANES), f32),
            pltpu.VMEM((n_tgt - 1, 2 * row_tiles, LANES), f32),
            pltpu.VMEM((col_tiles + 2, LANES), f32),
            pltpu.VMEM((n_src - 1, col_tiles + 2, LANES), f32),
            pltpu.VMEM((n_z, NX, owned, dim), f32),
            pltpu.VMEM((NX - 1, n_z, owned, dim), f32),
            pltpu.VMEM((n_z, owned, dim), f32),
            pltpu.VMEM((n_z - 1, owned, dim), f32),
            pltpu.SemaphoreType.DMA((3,)),
            pltpu.SemaphoreType.DMA((6,)),
            pltpu.SemaphoreType.DMA((6,)),
        ],
        compiler_params=pltpu.CompilerParams(
            collective_id=0, has_side_effects=True, vmem_limit_bytes=56 * 1024 * 1024
        ),
    )(
        src_embed, tgt_embed, qwen_embed,
        other_log.reshape(col_tiles, LANES),
        src_counts.reshape(row_tiles, LANES),
        tgt_counts.reshape(col_tiles, LANES),
    )


def solution(mesh):
    return jax.shard_map(
        functools.partial(on_device, mesh.shape["src"], mesh.shape["tgt"]),
        mesh=mesh,
        in_specs=(P("src", None), P("tgt", None), P("tgt", None), P("tgt"), P("src"), P("tgt")),
        out_specs=P(("src", "tgt"), None),
        check_vma=False,
    )
```

time: 647 us -> 85.9 us (0.13)
  blocking collectives: 391 us -> 0 us
  waiting for transfers between devices: 148 us -> 0 us
  Pallas kernels: 0 us -> 83.9 us
  other arithmetic: 68.7 us -> 0 us
  matrix products: 20.9 us -> 0 us
  between operations: 14.8 us -> 0.01 us
    psum x5 -> x0, blocking collectives: 201 us -> none  [the longest x2 141 us: row_lse(): total = lax.psum(jnp.sum(jnp.exp(values - peak[:, None]), axis=1), 'tgt')]
    pmax x4 -> x0, blocking collectives: 190 us -> none  [the longest x2 143 us: row_lse(): peak = lax.pmax(local_peak, 'tgt')]
    psum x1 -> x0, waiting for transfers between devices: 148 us -> none  [on_device(): summed = lax.psum(partial_rows, 'tgt')]
    pallas_call x0 -> x1, Pallas kernels: none -> 83.9 us  [on_device(): pl.pallas_call(functools.partial(kernel, n_src, n_tgt), out_shape=jax.Sha...]
    reduce_sum x6 -> x0, other arithmetic: 44 us -> none  [the longest x2 21.7 us: col_lse(): total = lax.psum(jnp.sum(jnp.exp(values - peak[None, :]), axis=0), 'src')]
    reduce_max x3 -> x0, other arithmetic: 24.6 us -> none  [the longest x2 16.6 us: col_lse(): local_peak = jnp.max(values, axis=0)]
    dot_general x2 -> x0, matrix products: 20.9 us -> none  [the longest x1 11.5 us: on_device(): jnp.dot(weights, qwen_embed, preferred_element_type=jnp.float32)]
  transfers between devices with their start and end apart: 1 -> 0, of which waited for: 1 -> 0; matrix products, arithmetic and copies ran while one was open for 0% -> 0% of each run, Pallas kernels for 0% -> 0%
where the time goes in v1:
time: 85.9 us; the launch traced here: 85.3 us
  Pallas kernels  83.9 us (98%)
  local copies, waits for them, and re-layouts  1.38 us (2%)
    pallas_call x1, Pallas kernels, on_device(): pl.pallas_call(functools.partial(kernel, n_src, n_tgt), out_shape=jax.Sha...  83.9 us

profile of v1, /device:TPU:32, one launch (start us, length us, event | category | flops | bytes accessed | tf_op | source)
XLA Modules:
  0.0 85.3 jit_solution(6826413980697330590)
XLA Ops:
  0.0 83.9 %shard_map.64 = f32[32,256]{1,0:T(8,128)} custom-call(bf16[1024,256]{1,0:T(8,128)(2,1)} %src_hbm.1, bf16[4864,256]{1,0:T(8,128)(2,1)} %tgt_hbm.1, bf16[4864,256]{1,0:T(8,128)(2,1)} %qwen_hbm.1, f32[38,128]{1,0:T(8,128)} %bitcast.3, s32[8,128]{1,0:T(8,128)} %bitcast.5, s32[38,128]{1,0:T(8,128)} %bitcast.4), custom_call_target="tpu_custom_call" | custom-call | tf_op jit(solution)/shard_map/pallas_call | solution.py:221
  83.9 1.4 %copy.8 = f32[32,256]{1,0:T(8,128)} copy(f32[32,256]{1,0:T(8,128)} %shard_map.64) | data formatting | bytes 65536

commit v2 on v1

v2 whole, which is shorter than its diff:
```python
import functools
import math

import jax
import jax.numpy as jnp
from jax import lax
from jax.experimental import pallas as pl
from jax.experimental.pallas import tpu as pltpu
from jax.sharding import PartitionSpec as P

MESH = pl.DeviceIdType.MESH
LANES = 128
WIDTH = 256
NX = 4
INV_TEMP = 4.0
SCALE = INV_TEMP * math.log2(math.e)
NT = (((1,), (1,)), ((), ()))
NN = (((1,), (0,)), ((), ()))


def dot(a, b, dims):
    return lax.dot_general(a, b, dims, preferred_element_type=jnp.float32)


def hops(d, n):
    return min(d, n - d)


def kernel(
    n_src, n_tgt,
    src_hbm, tgt_hbm, qwen_hbm, other_ref, src_counts_ref, tgt_counts_ref,
    out_ref,
    src_v, tgt_v, qwen_v, qt_v, logit_a, logit_b, kt_v, row_lhs, col_lhs, peak_v, gain_v,
    r1_send, r1_recv, t_send, t_recv, c1_send, c1_recv, r2_send, r2_recv, c2_send, c2_recv,
    f_send, hop_recv, relay_send, f_recv, g_send, g_recv,
    load_sem, send_sem, recv_sem, hop_sem, f_sem,
):
    rows = src_v.shape[0]
    cols = tgt_v.shape[0]
    n_z = n_tgt // NX
    row_tiles, col_tiles = rows // LANES, cols // LANES
    n_parts = rows // WIDTH
    me_src, me_tgt = lax.axis_index("src"), lax.axis_index("tgt")
    me_z, me_x = me_tgt // NX, me_tgt % NX

    n_blocks = 4
    block = cols // n_blocks
    step = block // 4

    def load_tgt(b):
        js = pl.ds(b * block, block)
        return pltpu.make_async_copy(tgt_hbm.at[js, :], tgt_v.at[js, :], load_sem.at[2 + b])

    load_src = pltpu.make_async_copy(src_hbm, src_v, load_sem.at[0])
    load_qwen = pltpu.make_async_copy(qwen_hbm, qwen_v, load_sem.at[1])
    load_src.start()
    for b in range(n_blocks):
        load_tgt(b).start()
    load_qwen.start()

    far = sorted(range(1, n_tgt), key=lambda d: -hops(d // NX, n_z) - hops(d % NX, NX))
    tgt_peers = [(me_src, (me_tgt + d) % n_tgt) for d in far]
    src_peers = [
        ((me_src + d) % n_src, me_tgt)
        for d in sorted(range(1, n_src), key=lambda d: -hops(d, n_src))
    ]
    barrier = pltpu.get_barrier_semaphore()
    for peer in tgt_peers + src_peers:
        pl.semaphore_signal(barrier, inc=1, device_id=peer, device_id_type=MESH)

    def send(src, dst, k, sem, peer):
        pltpu.make_async_remote_copy(
            src_ref=src, dst_ref=dst, send_sem=send_sem.at[k], recv_sem=sem,
            device_id=peer, device_id_type=MESH,
        ).start()

    def start(send_ref, recv_ref, k, peers):
        for slot, peer in enumerate(peers):
            send(send_ref, recv_ref.at[slot], k, recv_sem.at[k], peer)

    def wait(ref, sem):
        pltpu.make_async_copy(ref, ref, sem).wait()

    load_src.wait()

    def products(logit, i, js, peak):
        d = dot(tgt_v[js, :], src_v[i * WIDTH:(i + 1) * WIDTH, :], NT)
        logit[js, :] = d
        return jnp.maximum(peak, jnp.max(d.reshape(step // 8, 8, WIDTH), axis=0))

    def exponentials(logit, i, js, peak, total):
        e = jnp.exp2((logit[js, :] - peak) * SCALE)
        kt_v[js, i * WIDTH:(i + 1) * WIDTH] = e.astype(jnp.bfloat16)
        return total + jnp.sum(e.reshape(step // 8, 8, WIDTH), axis=0)

    def steps(b):
        for s in range(block // step):
            yield pl.ds(pl.multiple_of(b * block + s * step, step), step)

    low = jnp.full((8, WIDTH), -3.0e38, jnp.float32)
    zero = jnp.zeros((8, WIDTH), jnp.float32)
    logits = (logit_a, logit_b)

    def first(b, peak):
        load_tgt(b).wait()
        for js in steps(b):
            peak = products(logits[0], 0, js, peak)
        return peak

    peak = lax.fori_loop(0, n_blocks, first, low)
    for i in range(n_parts):
        peak = jnp.max(peak, axis=0, keepdims=True)

        def both(b, carry, peak=peak, i=i):
            later, total = carry
            for js in steps(b):
                if i + 1 < n_parts:
                    later = products(logits[(i + 1) % 2], i + 1, js, later)
                total = exponentials(logits[i % 2], i, js, peak, total)
            return later, total

        later, total = lax.fori_loop(0, n_blocks, both, (low, zero))
        lse = INV_TEMP * peak + jnp.log(jnp.sum(total, axis=0, keepdims=True))
        for h in range(WIDTH // LANES):
            t = i * (WIDTH // LANES) + h
            peak_v[t:t + 1, :] = peak[:, h * LANES:(h + 1) * LANES]
            r1_send[t:t + 1, :] = lse[:, h * LANES:(h + 1) * LANES]
        peak = later

    pl.semaphore_wait(barrier, len(tgt_peers) + len(src_peers))
    start(r1_send, r1_recv, 0, tgt_peers)

    tgt_counts = tgt_counts_ref[...].astype(jnp.float32)
    t_send[...] = jnp.full((1, LANES), jnp.sum(tgt_counts), jnp.float32)
    start(t_send, t_recv, 1, tgt_peers)
    other_mass = jnp.exp(other_ref[...])
    src_counts = src_counts_ref[...].astype(jnp.float32)
    row_lhs[...] = jnp.zeros_like(row_lhs)
    col_lhs[...] = jnp.zeros_like(col_lhs)
    c1_send[col_tiles:, :] = jnp.full((2, LANES), jnp.sum(src_counts), jnp.float32)
    load_qwen.wait()

    def turn(b, carry):
        js = pl.ds(pl.multiple_of(b * 256, 256), 256)
        qt_v[:, js] = qwen_v[js, :].T
        return carry

    lax.fori_loop(0, cols // 256, turn, 0)

    def spread(lhs, dense, tiles):
        high = dense.astype(jnp.bfloat16).astype(jnp.float32)
        rest = dense - high
        for t in range(tiles):
            lhs[0:1, t * LANES:(t + 1) * LANES] = high[t:t + 1, :]
            lhs[1:2, t * LANES:(t + 1) * LANES] = rest[t:t + 1, :]

    def column_sums(dest):
        a = row_lhs[...].astype(jnp.bfloat16)
        for b in range(cols // 256):
            c = jnp.sum(dot(a, kt_v[b * 256:(b + 1) * 256, :], NT), axis=0, keepdims=True)
            for h in range(2):
                dest[2 * b + h:2 * b + h + 1, :] = c[:, h * LANES:(h + 1) * LANES]

    wait(r1_recv, recv_sem.at[0])
    top = jnp.maximum(r1_send[...], jnp.max(r1_recv[...], axis=0))
    mass = jnp.exp(r1_send[...] - top) + jnp.sum(jnp.exp(r1_recv[...] - top), axis=0)
    factor = jnp.exp(INV_TEMP * peak_v[...] - (top + jnp.log(mass)))
    spread(row_lhs, src_counts * factor, row_tiles)

    column_sums(c1_send)
    start(c1_send, c1_recv, 2, src_peers)
    wait(t_recv, recv_sem.at[1])
    vocab_total = t_send[...] + jnp.sum(t_recv[...], axis=0)
    wait(c1_recv, recv_sem.at[2])
    sums = c1_send[...] + jnp.sum(c1_recv[...], axis=0)
    slab_total = sums[col_tiles:col_tiles + 1, :]
    spread(col_lhs, tgt_counts / (sums[:col_tiles, :] / slab_total + other_mass), col_tiles)

    r = jnp.sum(dot(col_lhs[...].astype(jnp.bfloat16), kt_v[...], NN), axis=0, keepdims=True)
    for t in range(row_tiles):
        r2_send[t:t + 1, :] = r[:, t * LANES:(t + 1) * LANES] * factor[t:t + 1, :]
    start(r2_send, r2_recv, 3, tgt_peers)
    wait(r2_recv, recv_sem.at[3])
    gain = factor / (r2_send[...] + jnp.sum(r2_recv[...], axis=0))
    gain_v[...] = gain
    spread(row_lhs, src_counts / slab_total * vocab_total * gain, row_tiles)

    column_sums(c2_send)
    start(c2_send, c2_recv, 4, src_peers)
    wait(c2_recv, recv_sem.at[4])
    sums = c2_send[...] + jnp.sum(c2_recv[...], axis=0)
    spread(col_lhs, tgt_counts / (sums + other_mass), col_tiles)

    for b in range(n_blocks):
        js = slice(b * block, (b + 1) * block)
        v = col_lhs[0:1, js] + col_lhs[1:2, js]
        qt_v[:, js] = (qt_v[:, js].astype(jnp.float32) * v).astype(jnp.bfloat16)

    right, left, across = (me_x + 1) % NX, (me_x + NX - 1) % NX, (me_x + 2) % NX
    to_right, to_left = (me_src, me_z * NX + right), (me_src, me_z * NX + left)
    order = sorted(range(n_parts), key=lambda k: -hops(k, n_parts))
    pair_of = [(me_z // 2 + d) % n_parts for d in order]

    def transport(k):
        lanes = pl.ds(pl.multiple_of(pair_of[k] * WIDTH, WIDTH), WIDTH)
        part = dot(qt_v[...], kt_v[:, lanes], NN)
        for h in range(2):
            scale = gain_v[pl.ds(pair_of[k] * 2 + h, 1), :]
            turned = (part[:, h * LANES:(h + 1) * LANES] * scale).T
            f_send[k, h] = turned.reshape(f_send.shape[2:])
        send(f_send.at[k, 0, across], hop_recv.at[k, 0], 5, hop_sem.at[k], to_right)
        send(f_send.at[k, 1, across], hop_recv.at[k, 1], 5, hop_sem.at[k], to_left)
        send(f_send.at[k, 1, right], f_recv.at[k, 0], 6, f_sem.at[k], to_right)
        send(f_send.at[k, 0, left], f_recv.at[k, 1], 6, f_sem.at[k], to_left)

    def relay(k):
        wait(hop_recv.at[k], hop_sem.at[k])
        relay_send[k, 0] = f_send[k, 0, right] + hop_recv[k, 0]
        relay_send[k, 1] = f_send[k, 1, left] + hop_recv[k, 1]
        send(relay_send.at[k, 0], f_recv.at[k, 2], 6, f_sem.at[k], to_right)
        send(relay_send.at[k, 1], f_recv.at[k, 3], 6, f_sem.at[k], to_left)

    def gather(k):
        wait(f_recv.at[k], f_sem.at[k])
        g_send[k, 0] = f_send[k, 0, me_x] + f_recv[k, 1] + f_recv[k, 2]
        g_send[k, 1] = f_send[k, 1, me_x] + f_recv[k, 0] + f_recv[k, 3]
        for h in range(2) if k < n_parts - 1 else [1 - me_z % 2]:
            z = pair_of[k] * 2 + h
            slot = (z - me_z + n_z) % n_z - 1
            send(g_send.at[k, h], g_recv.at[slot], 7, recv_sem.at[5], (me_src, z * NX + me_x))

    for k in range(n_parts + 2):
        if k < n_parts:
            transport(k)
        if 1 <= k <= n_parts:
            relay(k - 1)
        if k >= 2:
            gather(k - 2)

    wait(g_recv, recv_sem.at[5])
    out_ref[...] = g_send[n_parts - 1, me_z % 2] + jnp.sum(g_recv[...], axis=0)

    sent = (r1_recv, t_recv, c1_recv, r2_recv, c2_recv, hop_recv, f_recv, g_recv)
    for k, ref in enumerate(sent):
        wait(ref, send_sem.at[k])


def on_device(n_src, n_tgt, src_embed, tgt_embed, qwen_embed, other_log, src_counts, tgt_counts):
    rows, emb = src_embed.shape
    cols, dim = qwen_embed.shape
    row_tiles, col_tiles = rows // LANES, cols // LANES
    owned, n_z, n_parts = rows // n_tgt, n_tgt // NX, rows // WIDTH
    assert owned * NX == LANES and n_parts * 2 == n_z
    f32, bf16 = jnp.float32, jnp.bfloat16
    vmem = pl.BlockSpec(memory_space=pltpu.VMEM)
    hbm = pl.BlockSpec(memory_space=pl.ANY)
    return pl.pallas_call(
        functools.partial(kernel, n_src, n_tgt),
        out_shape=jax.ShapeDtypeStruct((owned, dim), f32),
        in_specs=[hbm, hbm, hbm, vmem, vmem, vmem],
        out_specs=vmem,
        scratch_shapes=[
            pltpu.VMEM((rows, emb), bf16),
            pltpu.VMEM((cols, emb), bf16),
            pltpu.VMEM((cols, dim), bf16),
            pltpu.VMEM((dim, cols), bf16),
            pltpu.VMEM((cols, WIDTH), f32),
            pltpu.VMEM((cols, WIDTH), f32),
            pltpu.VMEM((cols, rows), bf16),
            pltpu.VMEM((8, rows), f32),
            pltpu.VMEM((8, cols), f32),
            pltpu.VMEM((row_tiles, LANES), f32),
            pltpu.VMEM((row_tiles, LANES), f32),
            pltpu.VMEM((row_tiles, LANES), f32),
            pltpu.VMEM((n_tgt - 1, row_tiles, LANES), f32),
            pltpu.VMEM((1, LANES), f32),
            pltpu.VMEM((n_tgt - 1, 1, LANES), f32),
            pltpu.VMEM((col_tiles + 2, LANES), f32),
            pltpu.VMEM((n_src - 1, col_tiles + 2, LANES), f32),
            pltpu.VMEM((row_tiles, LANES), f32),
            pltpu.VMEM((n_tgt - 1, row_tiles, LANES), f32),
            pltpu.VMEM((col_tiles, LANES), f32),
            pltpu.VMEM((n_src - 1, col_tiles, LANES), f32),
            pltpu.VMEM((n_parts, 2, NX, owned, dim), f32),
            pltpu.VMEM((n_parts, 2, owned, dim), f32),
            pltpu.VMEM((n_parts, 2, owned, dim), f32),
            pltpu.VMEM((n_parts, 4, owned, dim), f32),
            pltpu.VMEM((n_parts, 2, owned, dim), f32),
            pltpu.VMEM((n_z - 1, owned, dim), f32),
            pltpu.SemaphoreType.DMA((6,)),
            pltpu.SemaphoreType.DMA((8,)),
            pltpu.SemaphoreType.DMA((6,)),
            pltpu.SemaphoreType.DMA((n_parts,)),
            pltpu.SemaphoreType.DMA((n_parts,)),
        ],
        compiler_params=pltpu.CompilerParams(
            collective_id=0, has_side_effects=True, vmem_limit_bytes=56 * 1024 * 1024
        ),
    )(
        src_embed, tgt_embed, qwen_embed,
        other_log.reshape(col_tiles, LANES),
        src_counts.reshape(row_tiles, LANES),
        tgt_counts.reshape(col_tiles, LANES),
    )


def solution(mesh):
    return jax.shard_map(
        functools.partial(on_device, mesh.shape["src"], mesh.shape["tgt"]),
        mesh=mesh,
        in_specs=(P("src", None), P("tgt", None), P("tgt", None), P("tgt"), P("src"), P("tgt")),
        out_specs=P(("src", "tgt"), None),
        check_vma=False,
    )
```

time: 85.9 us -> 64.9 us (0.76)
  Pallas kernels: 83.9 us -> 63.1 us
    pallas_call x1, Pallas kernels: 83.9 us -> 63.1 us  [on_device(): pl.pallas_call(functools.partial(kernel, n_src, n_tgt), out_shape=jax.Sha...]
where the time goes in v2:
time: 64.9 us; the launch traced here: 64.5 us
  Pallas kernels  63.1 us (97%)
  local copies, waits for them, and re-layouts  1.38 us (2%)
    pallas_call x1, Pallas kernels, on_device(): pl.pallas_call(functools.partial(kernel, n_src, n_tgt), out_shape=jax.Sha...  63.1 us
    unnamed x1, local copies, waits for them, and re-layouts  1.38 us

profile of v2, /device:TPU:32, one launch (start us, length us, event | category | flops | bytes accessed | tf_op | source)
XLA Modules:
  0.0 64.5 jit_solution(9256183902147162813)
XLA Ops:
  0.0 63.1 %shard_map.64 = f32[32,256]{1,0:T(8,128)} custom-call(bf16[1024,256]{1,0:T(8,128)(2,1)} %src_hbm.1, bf16[4864,256]{1,0:T(8,128)(2,1)} %tgt_hbm.1, bf16[4864,256]{1,0:T(8,128)(2,1)} %qwen_hbm.1, f32[38,128]{1,0:T(8,128)} %bitcast.3, s32[8,128]{1,0:T(8,128)} %bitcast.5, s32[38,128]{1,0:T(8,128)} %bitcast.4), custom_call_target="tpu_custom_call" | custom-call | tf_op jit(solution)/shard_map/pallas_call | solution.py:257
  63.1 1.4 %copy.8 = f32[32,256]{1,0:T(8,128)} copy(f32[32,256]{1,0:T(8,128)} %shard_map.64) | data formatting | bytes 65536

commit v3 on v2

--- a/solution.py
+++ b/solution.py
@@ -28,24 +28,27 @@
 
 def kernel(
     n_src, n_tgt,
-    src_hbm, tgt_hbm, qwen_hbm, other_ref, src_counts_ref, tgt_counts_ref,
+    src_hbm, tgt_hbm, qwen_hbm, other_hbm, src_counts_hbm, tgt_counts_hbm,
     out_ref,
-    src_v, tgt_v, qwen_v, qt_v, logit_a, logit_b, kt_v, row_lhs, col_lhs, peak_v, gain_v,
+    other_ref, src_counts_ref, tgt_counts_ref, src_v, tgt_v, qwen_v, qt_v, logit_a, logit_b, kt_v, row_lhs, col_lhs, peak_v, gain_v,
     r1_send, r1_recv, t_send, t_recv, c1_send, c1_recv, r2_send, r2_recv, c2_send, c2_recv,
-    f_send, hop_recv, relay_send, f_recv, g_send, g_recv,
-    load_sem, send_sem, recv_sem, hop_sem, f_sem,
+    f_send, f_recv, g_send, g_recv, d_recv,
+    load_sem, send_sem, recv_sem, f_sem,
 ):
     rows = src_v.shape[0]
     cols = tgt_v.shape[0]
     n_z = n_tgt // NX
     row_tiles, col_tiles = rows // LANES, cols // LANES
     n_parts = rows // WIDTH
+    width = logit_a.shape[1]
+    n_wide = rows // width
     me_src, me_tgt = lax.axis_index("src"), lax.axis_index("tgt")
     me_z, me_x = me_tgt // NX, me_tgt % NX
 
     n_blocks = 4
     block = cols // n_blocks
     step = block // 4
+    wide = cols // 4
 
     def load_tgt(b):
         js = pl.ds(b * block, block)
@@ -57,6 +60,13 @@
     for b in range(n_blocks):
         load_tgt(b).start()
     load_qwen.start()
+    load_small = [
+        pltpu.make_async_copy(src_counts_hbm, src_counts_ref, load_sem.at[6]),
+        pltpu.make_async_copy(tgt_counts_hbm, tgt_counts_ref, load_sem.at[7]),
+        pltpu.make_async_copy(other_hbm, other_ref, load_sem.at[8]),
+    ]
+    for load in load_small:
+        load.start()
 
     far = sorted(range(1, n_tgt), key=lambda d: -hops(d // NX, n_z) - hops(d % NX, NX))
     tgt_peers = [(me_src, (me_tgt + d) % n_tgt) for d in far]
@@ -84,45 +94,45 @@
     load_src.wait()
 
     def products(logit, i, js, peak):
-        d = dot(tgt_v[js, :], src_v[i * WIDTH:(i + 1) * WIDTH, :], NT)
+        d = dot(tgt_v[js, :], src_v[i * width:(i + 1) * width, :], NT)
         logit[js, :] = d
-        return jnp.maximum(peak, jnp.max(d.reshape(step // 8, 8, WIDTH), axis=0))
+        return jnp.maximum(peak, jnp.max(d.reshape(step // 8, 8, width), axis=0))
 
     def exponentials(logit, i, js, peak, total):
         e = jnp.exp2((logit[js, :] - peak) * SCALE)
-        kt_v[js, i * WIDTH:(i + 1) * WIDTH] = e.astype(jnp.bfloat16)
-        return total + jnp.sum(e.reshape(step // 8, 8, WIDTH), axis=0)
-
-    def steps(b):
-        for s in range(block // step):
-            yield pl.ds(pl.multiple_of(b * block + s * step, step), step)
-
-    low = jnp.full((8, WIDTH), -3.0e38, jnp.float32)
-    zero = jnp.zeros((8, WIDTH), jnp.float32)
+        kt_v[js, i * width:(i + 1) * width] = e.astype(jnp.bfloat16)
+        return total + jnp.sum(e.reshape(step // 8, 8, width), axis=0)
+
+    def steps(b, size):
+        for s in range(size // step):
+            yield pl.ds(pl.multiple_of(b * size + s * step, step), step)
+
+    low = jnp.full((8, width), -3.0e38, jnp.float32)
+    zero = jnp.zeros((8, width), jnp.float32)
     logits = (logit_a, logit_b)
 
     def first(b, peak):
         load_tgt(b).wait()
-        for js in steps(b):
+        for js in steps(b, block):
             peak = products(logits[0], 0, js, peak)
         return peak
 
     peak = lax.fori_loop(0, n_blocks, first, low)
-    for i in range(n_parts):
+    for i in range(n_wide):
         peak = jnp.max(peak, axis=0, keepdims=True)
 
         def both(b, carry, peak=peak, i=i):
             later, total = carry
-            for js in steps(b):
-                if i + 1 < n_parts:
+            for js in steps(b, wide):
+                if i + 1 < n_wide:
                     later = products(logits[(i + 1) % 2], i + 1, js, later)
                 total = exponentials(logits[i % 2], i, js, peak, total)
             return later, total
 
-        later, total = lax.fori_loop(0, n_blocks, both, (low, zero))
+        later, total = lax.fori_loop(0, 4, both, (low, zero))
         lse = INV_TEMP * peak + jnp.log(jnp.sum(total, axis=0, keepdims=True))
-        for h in range(WIDTH // LANES):
-            t = i * (WIDTH // LANES) + h
+        for h in range(width // LANES):
+            t = i * (width // LANES) + h
             peak_v[t:t + 1, :] = peak[:, h * LANES:(h + 1) * LANES]
             r1_send[t:t + 1, :] = lse[:, h * LANES:(h + 1) * LANES]
         peak = later
@@ -130,6 +140,8 @@
     pl.semaphore_wait(barrier, len(tgt_peers) + len(src_peers))
     start(r1_send, r1_recv, 0, tgt_peers)
 
+    for load in load_small:
+        load.wait()
     tgt_counts = tgt_counts_ref[...].astype(jnp.float32)
     t_send[...] = jnp.full((1, LANES), jnp.sum(tgt_counts), jnp.float32)
     start(t_send, t_recv, 1, tgt_peers)
@@ -154,12 +166,19 @@
             lhs[0:1, t * LANES:(t + 1) * LANES] = high[t:t + 1, :]
             lhs[1:2, t * LANES:(t + 1) * LANES] = rest[t:t + 1, :]
 
-    def column_sums(dest):
+    half = col_tiles // 16 * 8
+
+    def column_exchange(dest, recv_ref, k):
         a = row_lhs[...].astype(jnp.bfloat16)
         for b in range(cols // 256):
             c = jnp.sum(dot(a, kt_v[b * 256:(b + 1) * 256, :], NT), axis=0, keepdims=True)
             for h in range(2):
                 dest[2 * b + h:2 * b + h + 1, :] = c[:, h * LANES:(h + 1) * LANES]
+            if 2 * (b + 1) == half:
+                part = pl.ds(0, half)
+                start(dest.at[part], recv_ref.at[:, part], k, src_peers)
+        part = pl.ds(half, dest.shape[0] - half)
+        start(dest.at[part], recv_ref.at[:, part], k, src_peers)
 
     wait(r1_recv, recv_sem.at[0])
     top = jnp.maximum(r1_send[...], jnp.max(r1_recv[...], axis=0))
@@ -167,8 +186,7 @@
     factor = jnp.exp(INV_TEMP * peak_v[...] - (top + jnp.log(mass)))
     spread(row_lhs, src_counts * factor, row_tiles)
 
-    column_sums(c1_send)
-    start(c1_send, c1_recv, 2, src_peers)
+    column_exchange(c1_send, c1_recv, 2)
     wait(t_recv, recv_sem.at[1])
     vocab_total = t_send[...] + jnp.sum(t_recv[...], axis=0)
     wait(c1_recv, recv_sem.at[2])
@@ -185,8 +203,7 @@
     gain_v[...] = gain
     spread(row_lhs, src_counts / slab_total * vocab_total * gain, row_tiles)
 
-    column_sums(c2_send)
-    start(c2_send, c2_recv, 4, src_peers)
+    column_exchange(c2_send, c2_recv, 4)
     wait(c2_recv, recv_sem.at[4])
     sums = c2_send[...] + jnp.sum(c2_recv[...], axis=0)
     spread(col_lhs, tgt_counts / (sums + other_mass), col_tiles)
@@ -196,10 +213,11 @@
         v = col_lhs[0:1, js] + col_lhs[1:2, js]
         qt_v[:, js] = (qt_v[:, js].astype(jnp.float32) * v).astype(jnp.bfloat16)
 
-    right, left, across = (me_x + 1) % NX, (me_x + NX - 1) % NX, (me_x + 2) % NX
-    to_right, to_left = (me_src, me_z * NX + right), (me_src, me_z * NX + left)
     order = sorted(range(n_parts), key=lambda k: -hops(k, n_parts))
     pair_of = [(me_z // 2 + d) % n_parts for d in order]
+    n_first = f_recv.shape[0]
+    side = me_z % 2
+    xs = sorted(range(NX), key=lambda d: -hops(d, NX))
 
     def transport(k):
         lanes = pl.ds(pl.multiple_of(pair_of[k] * WIDTH, WIDTH), WIDTH)
@@ -208,39 +226,44 @@
             scale = gain_v[pl.ds(pair_of[k] * 2 + h, 1), :]
             turned = (part[:, h * LANES:(h + 1) * LANES] * scale).T
             f_send[k, h] = turned.reshape(f_send.shape[2:])
-        send(f_send.at[k, 0, across], hop_recv.at[k, 0], 5, hop_sem.at[k], to_right)
-        send(f_send.at[k, 1, across], hop_recv.at[k, 1], 5, hop_sem.at[k], to_left)
-        send(f_send.at[k, 1, right], f_recv.at[k, 0], 6, f_sem.at[k], to_right)
-        send(f_send.at[k, 0, left], f_recv.at[k, 1], 6, f_sem.at[k], to_left)
-
-    def relay(k):
-        wait(hop_recv.at[k], hop_sem.at[k])
-        relay_send[k, 0] = f_send[k, 0, right] + hop_recv[k, 0]
-        relay_send[k, 1] = f_send[k, 1, left] + hop_recv[k, 1]
-        send(relay_send.at[k, 0], f_recv.at[k, 2], 6, f_sem.at[k], to_right)
-        send(relay_send.at[k, 1], f_recv.at[k, 3], 6, f_sem.at[k], to_left)
-
-    def gather(k):
+
+    def over_x(k):
+        for d in xs[:-1]:
+            x = (me_x + d) % NX
+            send(f_send.at[k, :, x], f_recv.at[k, d - 1], 5, f_sem.at[k], (me_src, me_z * NX + x))
+
+    def over_z(k):
         wait(f_recv.at[k], f_sem.at[k])
-        g_send[k, 0] = f_send[k, 0, me_x] + f_recv[k, 1] + f_recv[k, 2]
-        g_send[k, 1] = f_send[k, 1, me_x] + f_recv[k, 0] + f_recv[k, 3]
-        for h in range(2) if k < n_parts - 1 else [1 - me_z % 2]:
-            z = pair_of[k] * 2 + h
-            slot = (z - me_z + n_z) % n_z - 1
-            send(g_send.at[k, h], g_recv.at[slot], 7, recv_sem.at[5], (me_src, z * NX + me_x))
-
-    for k in range(n_parts + 2):
-        if k < n_parts:
-            transport(k)
-        if 1 <= k <= n_parts:
-            relay(k - 1)
-        if k >= 2:
-            gather(k - 2)
+        g_send[k] = f_send[k, :, me_x] + jnp.sum(f_recv[k], axis=0)
+        for h in range(2):
+            owner = (me_src, (pair_of[k] * 2 + h) * NX + me_x)
+            send(g_send.at[k, h], g_recv.at[2 * k + side], 6, recv_sem.at[5], owner)
+
+    def straight(k):
+        for d in xs:
+            x = (me_x + d) % NX
+            for h in range(2):
+                if h == 0 and d == 0:
+                    continue
+                half = (side + h) % 2
+                owner = (me_src, (pair_of[k] * 2 + half) * NX + x)
+                send(f_send.at[k, half, x], d_recv.at[h * NX + d - 1], 7, recv_sem.at[6], owner)
+
+    for k in range(n_parts):
+        transport(k)
+        if k < n_first:
+            over_x(k)
+    for k in range(n_first):
+        if k == n_first - 1:
+            straight(n_parts - 1)
+        over_z(k)
 
     wait(g_recv, recv_sem.at[5])
-    out_ref[...] = g_send[n_parts - 1, me_z % 2] + jnp.sum(g_recv[...], axis=0)
-
-    sent = (r1_recv, t_recv, c1_recv, r2_recv, c2_recv, hop_recv, f_recv, g_recv)
+    wait(d_recv, recv_sem.at[6])
+    total = f_send[n_parts - 1, side, me_x] + jnp.sum(d_recv[...], axis=0)
+    out_ref[...] = total + jnp.sum(g_recv[...], axis=0)
+
+    sent = (r1_recv, t_recv, c1_recv, r2_recv, c2_recv, f_recv, g_recv, d_recv)
     for k, ref in enumerate(sent):
         wait(ref, send_sem.at[k])
 
@@ -251,21 +274,25 @@
     row_tiles, col_tiles = rows // LANES, cols // LANES
     owned, n_z, n_parts = rows // n_tgt, n_tgt // NX, rows // WIDTH
     assert owned * NX == LANES and n_parts * 2 == n_z
+    n_first = n_parts - 1
     f32, bf16 = jnp.float32, jnp.bfloat16
     vmem = pl.BlockSpec(memory_space=pltpu.VMEM)
-    hbm = pl.BlockSpec(memory_space=pl.ANY)
+    hbm = pl.BlockSpec(memory_space=pltpu.HBM)
     return pl.pallas_call(
         functools.partial(kernel, n_src, n_tgt),
         out_shape=jax.ShapeDtypeStruct((owned, dim), f32),
-        in_specs=[hbm, hbm, hbm, vmem, vmem, vmem],
+        in_specs=[hbm] * 6,
         out_specs=vmem,
         scratch_shapes=[
+            pltpu.VMEM((col_tiles, LANES), f32),
+            pltpu.VMEM((row_tiles, LANES), jnp.int32),
+            pltpu.VMEM((col_tiles, LANES), jnp.int32),
             pltpu.VMEM((rows, emb), bf16),
             pltpu.VMEM((cols, emb), bf16),
             pltpu.VMEM((cols, dim), bf16),
             pltpu.VMEM((dim, cols), bf16),
-            pltpu.VMEM((cols, WIDTH), f32),
-            pltpu.VMEM((cols, WIDTH), f32),
+            pltpu.VMEM((cols, min(512, rows)), f32),
+            pltpu.VMEM((cols, min(512, rows)), f32),
             pltpu.VMEM((cols, rows), bf16),
             pltpu.VMEM((8, rows), f32),
             pltpu.VMEM((8, cols), f32),
@@ -282,16 +309,14 @@
             pltpu.VMEM((col_tiles, LANES), f32),
             pltpu.VMEM((n_src - 1, col_tiles, LANES), f32),
             pltpu.VMEM((n_parts, 2, NX, owned, dim), f32),
-            pltpu.VMEM((n_parts, 2, owned, dim), f32),
-            pltpu.VMEM((n_parts, 2, owned, dim), f32),
-            pltpu.VMEM((n_parts, 4, owned, dim), f32),
-            pltpu.VMEM((n_parts, 2, owned, dim), f32),
-            pltpu.VMEM((n_z - 1, owned, dim), f32),
-            pltpu.SemaphoreType.DMA((6,)),
+            pltpu.VMEM((n_first, NX - 1, 2, owned, dim), f32),
+            pltpu.VMEM((n_first, 2, owned, dim), f32),
+            pltpu.VMEM((2 * n_first, owned, dim), f32),
+            pltpu.VMEM((2 * NX - 1, owned, dim), f32),
+            pltpu.SemaphoreType.DMA((9,)),
             pltpu.SemaphoreType.DMA((8,)),
-            pltpu.SemaphoreType.DMA((6,)),
-            pltpu.SemaphoreType.DMA((n_parts,)),
-            pltpu.SemaphoreType.DMA((n_parts,)),
+            pltpu.SemaphoreType.DMA((7,)),
+            pltpu.SemaphoreType.DMA((n_first,)),
         ],
         compiler_params=pltpu.CompilerParams(
             collective_id=0, has_side_effects=True, vmem_limit_bytes=56 * 1024 * 1024

time: 64.9 us -> 62 us (0.955)
  Pallas kernels: 63.1 us -> 60.5 us
    pallas_call x1, Pallas kernels: 63.1 us -> 60.5 us  [on_device(): pl.pallas_call(functools.partial(kernel, n_src, n_tgt), out_shape=jax.Sha...]
where the time goes in v3:
time: 62 us; the launch traced here: 61.9 us
  Pallas kernels  60.5 us (98%)
  local copies, waits for them, and re-layouts  1.38 us (2%)
    pallas_call x1, Pallas kernels, on_device(): pl.pallas_call(functools.partial(kernel, n_src, n_tgt), out_shape=jax.Sha...  60.5 us
    unnamed x1, local copies, waits for them, and re-layouts  1.38 us

profile of v3, /device:TPU:32, one launch (start us, length us, event | category | flops | bytes accessed | tf_op | source)
XLA Modules:
  0.0 61.9 jit_solution(10355099161206860320)
XLA Ops:
  0.0 60.5 %shard_map.64 = f32[32,256]{1,0:T(8,128)} custom-call(bf16[1024,256]{1,0:T(8,128)(2,1)} %src_hbm.1, bf16[4864,256]{1,0:T(8,128)(2,1)} %tgt_hbm.1, bf16[4864,256]{1,0:T(8,128)(2,1)} %qwen_hbm.1, f32[38,128]{1,0:T(8,128)} %bitcast.3, s32[8,128]{1,0:T(8,128)} %bitcast.5, s32[38,128]{1,0:T(8,128)} %bitcast.4), custom_call_target="tpu_custom_call" | custom-call | tf_op jit(solution)/shard_map/pallas_call | solution.py:281
  60.5 1.4 %copy.8 = f32[32,256]{1,0:T(8,128)} copy(f32[32,256]{1,0:T(8,128)} %shard_map.64) | data formatting | bytes 65536

commit v4 on v3

--- a/solution.py
+++ b/solution.py
@@ -59,7 +59,6 @@
     load_src.start()
     for b in range(n_blocks):
         load_tgt(b).start()
-    load_qwen.start()
     load_small = [
         pltpu.make_async_copy(src_counts_hbm, src_counts_ref, load_sem.at[6]),
         pltpu.make_async_copy(tgt_counts_hbm, tgt_counts_ref, load_sem.at[7]),
@@ -118,6 +117,7 @@
         return peak
 
     peak = lax.fori_loop(0, n_blocks, first, low)
+    load_qwen.start()
     for i in range(n_wide):
         peak = jnp.max(peak, axis=0, keepdims=True)
 

time: 62 us -> 62 us (level)
  no operation moved by 1% of the time
where the time goes in v4:
time: 62 us; the launch traced here: 61.9 us
  Pallas kernels  60.5 us (98%)
  local copies, waits for them, and re-layouts  1.38 us (2%)
    pallas_call x1, Pallas kernels, on_device(): pl.pallas_call(functools.partial(kernel, n_src, n_tgt), out_shape=jax.Sha...  60.5 us
    unnamed x1, local copies, waits for them, and re-layouts  1.38 us

profile of v4, /device:TPU:32, one launch (start us, length us, event | category | flops | bytes accessed | tf_op | source)
XLA Modules:
  0.0 61.9 jit_solution(16919632587224077018)
XLA Ops:
  0.0 60.5 %shard_map.64 = f32[32,256]{1,0:T(8,128)} custom-call(bf16[1024,256]{1,0:T(8,128)(2,1)} %src_hbm.1, bf16[4864,256]{1,0:T(8,128)(2,1)} %tgt_hbm.1, bf16[4864,256]{1,0:T(8,128)(2,1)} %qwen_hbm.1, f32[38,128]{1,0:T(8,128)} %bitcast.3, s32[8,128]{1,0:T(8,128)} %bitcast.5, s32[38,128]{1,0:T(8,128)} %bitcast.4), custom_call_target="tpu_custom_call" | custom-call | tf_op jit(solution)/shard_map/pallas_call | solution.py:281
  60.5 1.4 %copy.8 = f32[32,256]{1,0:T(8,128)} copy(f32[32,256]{1,0:T(8,128)} %shard_map.64) | data formatting | bytes 65536

commit v5 on v4

--- a/solution.py
+++ b/solution.py
@@ -144,7 +144,6 @@
         load.wait()
     tgt_counts = tgt_counts_ref[...].astype(jnp.float32)
     t_send[...] = jnp.full((1, LANES), jnp.sum(tgt_counts), jnp.float32)
-    start(t_send, t_recv, 1, tgt_peers)
     other_mass = jnp.exp(other_ref[...])
     src_counts = src_counts_ref[...].astype(jnp.float32)
     row_lhs[...] = jnp.zeros_like(row_lhs)
@@ -187,8 +186,7 @@
     spread(row_lhs, src_counts * factor, row_tiles)
 
     column_exchange(c1_send, c1_recv, 2)
-    wait(t_recv, recv_sem.at[1])
-    vocab_total = t_send[...] + jnp.sum(t_recv[...], axis=0)
+    start(t_send, t_recv, 1, tgt_peers)
     wait(c1_recv, recv_sem.at[2])
     sums = c1_send[...] + jnp.sum(c1_recv[...], axis=0)
     slab_total = sums[col_tiles:col_tiles + 1, :]
@@ -198,6 +196,8 @@
     for t in range(row_tiles):
         r2_send[t:t + 1, :] = r[:, t * LANES:(t + 1) * LANES] * factor[t:t + 1, :]
     start(r2_send, r2_recv, 3, tgt_peers)
+    wait(t_recv, recv_sem.at[1])
+    vocab_total = t_send[...] + jnp.sum(t_recv[...], axis=0)
     wait(r2_recv, recv_sem.at[3])
     gain = factor / (r2_send[...] + jnp.sum(r2_recv[...], axis=0))
     gain_v[...] = gain

time: 62 us -> 61.7 us (level)
  no operation moved by 1% of the time
where the time goes in v5:
time: 61.7 us; the launch traced here: 61.4 us
  Pallas kernels  60 us (97%)
  local copies, waits for them, and re-layouts  1.38 us (2%)
    pallas_call x1, Pallas kernels, on_device(): pl.pallas_call(functools.partial(kernel, n_src, n_tgt), out_shape=jax.Sha...  60 us
    unnamed x1, local copies, waits for them, and re-layouts  1.38 us

profile of v5, /device:TPU:32, one launch (start us, length us, event | category | flops | bytes accessed | tf_op | source)
XLA Modules:
  0.0 61.4 jit_solution(6955022723810413796)
XLA Ops:
  0.0 60.0 %shard_map.64 = f32[32,256]{1,0:T(8,128)} custom-call(bf16[1024,256]{1,0:T(8,128)(2,1)} %src_hbm.1, bf16[4864,256]{1,0:T(8,128)(2,1)} %tgt_hbm.1, bf16[4864,256]{1,0:T(8,128)(2,1)} %qwen_hbm.1, f32[38,128]{1,0:T(8,128)} %bitcast.3, s32[8,128]{1,0:T(8,128)} %bitcast.5, s32[38,128]{1,0:T(8,128)} %bitcast.4), custom_call_target="tpu_custom_call" | custom-call | tf_op jit(solution)/shard_map/pallas_call | solution.py:281
  60.0 1.4 %copy.8 = f32[32,256]{1,0:T(8,128)} copy(f32[32,256]{1,0:T(8,128)} %shard_map.64) | data formatting | bytes 65536
